TPU v7x, 512 devices: a whole 4x4x16 slice. The times are simulated.
512 devices in a mesh: ctx: 64 (over y, z), head: 8 (over x, core).
Axes of the slice: x: 4, y: 4, z: 16, core: 2. Of those that a mesh axis runs over, the one named last changes fastest.
Arguments:
- lin_query: bfloat16 [8192, 64, 128], P('ctx', 'head'), may hold values from -6 to 6
- lin_key: bfloat16 [8192, 64, 128], P('ctx', 'head'), may hold values from -6 to 6
- lin_value: bfloat16 [8192, 64, 128], P('ctx', 'head'), may hold values from -18 to 18
- log_decay: float32 [64, 8192], P('head', 'ctx'), may hold values from -1 to 0
- norm_gain: float32 [64, 128], P('head'), may hold values from 0.5 to 1.5
- attn_query: bfloat16 [8192, 64, 128], P('ctx', 'head'), may hold values from -30 to 30
- attn_key: bfloat16 [8192, 8, 128], P('ctx', 'head'), may hold values from -16 to 16
- attn_value: bfloat16 [8192, 8, 128], P('ctx', 'head'), may hold values from -6 to 6
Outputs:
- lin_out: bfloat16 [8192, 64, 128], P('ctx', 'head')
- attn_out: bfloat16 [8192, 64, 128], P('ctx', 'head')
All inputs are finite; a program needn't handle non-finite values.
Results may differ from a plain program's by a relative error of at most 0.0055.
Values may be sent and summed in bfloat16 or wider, within the bound.
No kernel may reach another device: no remote copies, remote signals or barrier semaphores. Data moves between devices by JAX's collectives and lax.ppermute only.
A program may use at most 192 MiB of HBM per device.

v0:
```python
import jax
import jax.numpy as jnp
from jax import lax
from jax.sharding import PartitionSpec as P

QUERY_HEADS = 64
HD = 128


def carried_in(x, axis, combine, identity):
    size, mine = (lax.axis_size(axis), lax.axis_index(axis))
    everything = jax.tree.map(lambda part: lax.all_gather(part, axis), x)
    start = jax.tree.map(
        lambda part, zero: jnp.broadcast_to(jnp.asarray(zero, part.dtype), part.shape), x, identity
    )

    def hop(k, before):
        reached = k < mine
        new = combine(before, jax.tree.map(lambda part: part[k], everything))
        return jax.tree.map(lambda a, b: jnp.where(reached, a, b), new, before)

    return lax.fori_loop(0, size, hop, start)


def act_round(values):
    return jax.nn.silu(values.astype(jnp.float32)).astype(jnp.bfloat16)


def chain_state(earlier, later):
    decay_early, state_early = earlier
    decay_late, state_late = later
    return (decay_early * decay_late, decay_late[:, None, None] * state_early + state_late)


def lightning(lin_query, lin_key, lin_value, log_decay, norm_gain):
    act_query = act_round(lin_query)
    act_key = act_round(lin_key)
    act_value = act_round(lin_value)
    token_position = jnp.arange(lin_query.shape[0])
    cumulative = jnp.cumsum(log_decay, axis=1)
    causal = token_position[:, None] >= token_position[None, :]
    spread = cumulative[:, :, None] - cumulative[:, None, :]
    decay_matrix = jnp.exp(jnp.where(causal[None], spread, -1e30))
    scores = jnp.einsum("thd,shd->hts", act_query, act_key, preferred_element_type=jnp.float32)
    weights = (scores * decay_matrix).astype(jnp.bfloat16)
    inner_part = jnp.einsum("hts,shd->thd", weights, act_value, preferred_element_type=jnp.float32)
    last_sum = cumulative[:, -1]
    key_factor = jnp.exp(last_sum[None, :] - cumulative.T)
    scaled_keys = (act_key.astype(jnp.float32) * key_factor[:, :, None]).astype(jnp.bfloat16)
    local_state = jnp.einsum(
        "shd,she->hde", scaled_keys, act_value, preferred_element_type=jnp.float32
    )
    identity = (jnp.ones_like(last_sum), jnp.zeros_like(local_state))
    prior_decay, prior_state = carried_in(
        (jnp.exp(last_sum), local_state), "ctx", chain_state, identity
    )
    outer_part = jnp.einsum(
        "thd,hde->the", act_query.astype(jnp.float32), prior_state, precision=lax.Precision.HIGHEST
    )
    mixed_out = inner_part + outer_part * jnp.exp(cumulative.T)[:, :, None]
    row_squares = jnp.sum(mixed_out * mixed_out, axis=(1, 2))
    total_squares = lax.psum(row_squares, "head")
    inverse = lax.rsqrt(total_squares / (QUERY_HEADS * HD) + 1e-06)
    return (mixed_out * inverse[:, None, None] * norm_gain[None]).astype(jnp.bfloat16)


def to_groups(query_rows, kv_local):
    rows = query_rows.shape[0]
    group = query_rows.shape[1] // kv_local
    shaped = query_rows.reshape(rows, kv_local, group, query_rows.shape[2]).transpose(1, 0, 2, 3)
    return shaped.reshape(kv_local, rows * group, query_rows.shape[2])


def from_groups(grouped, rows):
    kv_local = grouped.shape[0]
    group = grouped.shape[1] // rows
    shaped = grouped.reshape(kv_local, rows, group, grouped.shape[2]).transpose(1, 0, 2, 3)
    return shaped.reshape(rows, kv_local * group, grouped.shape[2])


def attend(state_now, group_query, positions, key_piece, value_piece):
    running_max, totals, accumulated = state_now
    scores = jnp.einsum(
        "gqd,pgd->gqp", group_query, key_piece, preferred_element_type=jnp.float32
    ) * HD ** (-0.5)
    key_pos = jnp.arange(key_piece.shape[0])
    visible = positions[:, None] >= key_pos[None, :]
    masked = jnp.where(visible[None], scores, -1e30)
    newest = jnp.maximum(running_max, jnp.max(masked, axis=2))
    prob_rows = jnp.where(visible[None], jnp.exp(scores - newest[:, :, None]), 0.0)
    totals = jnp.sum(prob_rows, axis=2)
    accumulated = jnp.einsum(
        "gqp,pgd->gqd",
        prob_rows.astype(jnp.bfloat16),
        value_piece,
        preferred_element_type=jnp.float32,
    )
    return (newest, totals, accumulated)


def softmax_part(attn_query, attn_key, attn_value):
    length = attn_query.shape[0]
    kv_local = attn_key.shape[1]
    group = attn_query.shape[1] // kv_local
    ctx_index = lax.axis_index("ctx")
    own_pos = ctx_index * length + jnp.arange(length)
    query_sets = [(to_groups(attn_query, kv_local), jnp.repeat(own_pos, group), length)]

    def empty_state(group_query):
        shape_rows = group_query.shape[:2]
        return (
            jnp.full(shape_rows, -1e30, jnp.float32),
            jnp.zeros(shape_rows, jnp.float32),
            jnp.zeros(group_query.shape, jnp.float32),
        )

    initial = tuple((empty_state(query_set[0]) for query_set in query_sets))
    key_piece = lax.all_gather(attn_key, "ctx", axis=0, tiled=True)
    value_piece = lax.all_gather(attn_value, "ctx", axis=0, tiled=True)
    results = []
    for query_set, state_now in zip(query_sets, initial):
        group_query, positions, set_rows = query_set
        state_now = attend(state_now, group_query, positions, key_piece, value_piece)
        results.append(state_now)
    finals = tuple(results)
    running_max, totals, accumulated = finals[0]
    grouped = (accumulated / totals[:, :, None]).astype(jnp.bfloat16)
    result = from_groups(grouped, length)
    return result


def local(lin_query, lin_key, lin_value, log_decay, norm_gain, attn_query, attn_key, attn_value):
    lin_out = lightning(lin_query, lin_key, lin_value, log_decay, norm_gain)
    attn_out = softmax_part(attn_query, attn_key, attn_value)
    return (lin_out, attn_out)


def solution(mesh):
    return jax.shard_map(
        local,
        mesh=mesh,
        in_specs=(
            P("ctx", "head", None),
            P("ctx", "head", None),
            P("ctx", "head", None),
            P("head", "ctx"),
            P("head", None),
            P("ctx", "head", None),
            P("ctx", "head", None),
            P("ctx", "head", None),
        ),
        out_specs=(P("ctx", "head", None), P("ctx", "head", None)),
        check_vma=False,
    )
```

profile of v0, /device:TPU:1, one launch (start us, length us, event | category | flops | bytes accessed | tf_op | source)
XLA Modules:
  0.0 689.5 jit_solution(787471788955299901)
XLA Ops:
  10.0 1.4 multiply_convert_fusion.1
  12.5 1.3 dynamic-slice
  14.7 123.1 %all-reduce = f32[512]{0:T(512)S(1)} all-reduce(f32[512]{0:T(512)S(1)} %dynamic-update-slice), channel_id=2, replica_groups=mesh['ctx'=64,'head'=8] {'ctx'}, use_global_device_ids=true, to_apply=%add | all-reduce | flops 512 | bytes 4096
  139.3 9.0 %all-gather.6.cloned.1.call-done = bf16[8192,1,128]{2,0,1:T(8,128)(2,1)} async-done(((bf16[128,1,128]{2,0,1:T(8,128)(2,1)}), bf16[8192,1,128]{2,0,1:T(8,128)(2,1)}) %all-gather.6.cloned.1.call-update) | async-done | bytes 2097168 | tf_op jit(solution)/shard_map/all_gather | solution.py:118
  148.3 15.5 %select_reduce_fusion = (f32[1024]{0:T(1024)S(1)}, f32[1024,8192]{1,0:T(8,128)}) fusion(s32[1024]{0:T(1024)S(1)} %ge.35, bf16[8192,1,128]{2,0,1:T(8,128)(2,1)} %all-gather.6.cloned.1.call-done, bf16[128,8,128]{2,1,0:T(8,128)(2,1)S(1)} %copy-done), kind=kOutput, calls=%fused_computation.4 | convolution fusion | flops 2181037056 | bytes 35921920 | tf_op jit(solution)/shard_map/gqd,pgd->gqp/dot_general | solution.py:83
  163.8 15.6 %fusion.1 = f32[1024]{0:T(1024)S(1)} fusion(f32[1024,8192]{1,0:T(8,128)} %get-tuple-element.140, f32[1024]{0:T(1024)S(1)} %broadcast_maximum_fusion, s32[1024]{0:T(1024)S(1)} %ge.35), kind=kLoop, calls=%fused_computation.6 | loop fusion | flops 41942016 | bytes 33566720 | tf_op jit(solution)/shard_map/reduce_sum | solution.py:91
  179.4 108.9 %all-gather.8.cloned.1.call-done = bf16[8192,1,128]{2,0,1:T(8,128)(2,1)} async-done(((bf16[128,1,128]{2,0,1:T(8,128)(2,1)}), bf16[8192,1,128]{2,0,1:T(8,128)(2,1)}) %all-gather.8.cloned.1.call-update) | async-done | bytes 2097168 | tf_op jit(solution)/shard_map/all_gather | solution.py:119
  288.3 15.6 %fusion.21 = bf16[128,8,128]{2,1,0:T(8,128)(2,1)} fusion(bf16[8192,1,128]{2,0,1:T(8,128)(2,1)} %all-gather.8.cloned.1.call-done, f32[1024,8192]{1,0:T(8,128)} %get-tuple-element.140, f32[1024]{0:T(1024)S(1)} %broadcast_maximum_fusion, s32[1024]{0:T(1024)S(1)} %ge.35, f32[1024]{0:T(1024)S(1)} %fusion.1), kind=kOutput, calls=%fused_computation.20 | convolution fusion | flops 2189688832 | bytes 35926016 | tf_op jit(solution)/shard_map/gqp,pgd->gqd/dot_general | solution.py:92
  303.8 286.3 %all-gather.10.cloned.1.call-done = f32[512,128,128]{2,1,0:T(8,128)} async-done(((f32[8,128,128]{2,1,0:T(8,128)}), f32[512,128,128]{2,1,0:T(8,128)}) %all-gather.10.cloned.1.call-update) | async-done | bytes 33554448 | tf_op jit(solution)/shard_map/all_gather | solution.py:12
  590.1 77.7 %while.14 = (s32[]{:T(128)}, f32[8,128,128]{2,1,0:T(8,128)S(1)}, s32[]{:T(128)}, f32[64,8]{1,0:T(8,128)S(1)}, f32[64,8,128,128]{3,2,1,0:T(8,128)}, /*index=5*/s32[]{:T(128)}, s32[]{:T(128)}) while((s32[]{:T(128)}, f32[8,128,128]{2,1,0:T(8,128)S(1)}, s32[]{:T(128)}, f32[64,8]{1,0:T(8,128)S(1)}, f32[64,8,128,128]{3,2,1,0:T(8,128)}, ...), condition=%wide.region_2.3_spmd.clone, body=%wide.region_1.2_spmd.clone.sunk | while | flops 524292 | bytes 1573065 | solution.py:22
  591.4 1.2 fusion.65
  592.6 1.2 fusion.65
  593.8 1.2 fusion.65
  595.0 1.2 fusion.65
  596.2 1.2 fusion.65
  597.4 1.2 fusion.65
  598.6 1.2 fusion.65
  599.9 1.2 fusion.65
  602.3 1.2 fusion.65
  604.7 1.2 fusion.65
  605.9 1.2 fusion.65
  607.1 1.2 fusion.65
  608.4 1.2 fusion.65
  609.6 1.2 fusion.65
  610.8 1.2 fusion.65
  612.0 1.2 fusion.65
  613.2 1.2 fusion.65
  614.4 1.2 fusion.65
  615.6 1.2 fusion.65
  616.8 1.2 fusion.65
  618.1 1.2 fusion.65
  619.3 1.2 fusion.65
  620.5 1.2 fusion.65
  621.7 1.2 fusion.65
  622.9 1.2 fusion.65
  625.3 1.2 fusion.65
  627.8 1.2 fusion.65
  629.0 1.2 fusion.65
  630.2 1.2 fusion.65
  631.4 1.2 fusion.65
  632.6 1.2 fusion.65
  633.8 1.2 fusion.65
  635.1 1.2 fusion.65
  636.3 1.2 fusion.65
  637.5 1.2 fusion.65
  638.7 1.2 fusion.65
  639.9 1.2 fusion.65
  641.1 1.2 fusion.65
  642.3 1.2 fusion.65
  643.6 1.2 fusion.65
  644.8 1.2 fusion.65
  646.0 1.2 fusion.65
  648.4 1.2 fusion.65
  650.8 1.2 fusion.65
  652.1 1.2 fusion.65
  653.3 1.2 fusion.65
  654.5 1.2 fusion.65
  655.7 1.2 fusion.65
  656.9 1.2 fusion.65
  658.1 1.2 fusion.65
  659.3 1.2 fusion.65
  660.6 1.2 fusion.65
  661.8 1.2 fusion.65
  669.0 12.9 %psum.7 = f32[128]{0:T(128)S(1)} all-reduce(f32[128]{0:T(128)S(1)} %get-tuple-element.137), channel_id=1, replica_groups=mesh['ctx'=64,'head'=8] {'head'}, use_global_device_ids=true, to_apply=%region_4.5 | all-reduce | flops 128 | bytes 1024 | tf_op jit(solution)/shard_map/psum | solution.py:62
  (107 shorter events, 21.3 us)
Async XLA Ops:
  7.2 141.1 %copy-start = (bf16[128,8,128]{2,1,0:T(8,128)(2,1)S(1)}, bf16[128,8,128]{2,1,0:T(8,128)(2,1)}, u32[]{:S(2)}) copy-start(bf16[128,8,128]{2,1,0:T(8,128)(2,1)} %param.15) | copy-start | bytes 786436
  7.2 141.1 %all-gather.6.cloned.1.call-start = ((), (), s32[]{:S(2)}) async-start(), calls=%async_computation | async-start | bytes 2129920 | tf_op jit(solution)/shard_map/all_gather | solution.py:118
  7.9 280.4 %all-gather.8.cloned.1.call-start = ((), (), s32[]{:S(2)}) async-start(), calls=%async_computation.1 | async-start | bytes 2129920 | tf_op jit(solution)/shard_map/all_gather | solution.py:119
  8.7 581.5 %all-gather.10.cloned.1.call-start = ((), (), s32[]{:S(2)}) async-start(), calls=%async_computation.2 | async-start | bytes 34078720 | tf_op jit(solution)/shard_map/all_gather | solution.py:12
  163.8 519.2 %copy-start.1 = (bf16[128,8,128]{2,1,0:T(8,128)(2,1)S(1)}, bf16[128,8,128]{2,1,0:T(8,128)(2,1)}, u32[]{:S(2)}) copy-start(bf16[128,8,128]{2,1,0:T(8,128)(2,1)} %param.15) | copy-start | bytes 786436
  179.4 502.4 %copy-start.2 = (f32[8,128]{1,0:T(8,128)S(1)}, f32[8,128]{1,0:T(8,128)}, u32[]{:S(2)}) copy-start(f32[8,128]{1,0:T(8,128)} %param.14) | copy-start | bytes 12292
Sparse Core Ops, SparseCore 0:
  11.0 137.2 all-gather.5
  151.2 136.9 all-gather.7
  291.2 298.8 all-gather.9
where the time goes:
time: 693 us; the launch traced here: 689 us
  waiting for transfers between devices  406 us (59%)
  blocking collectives  136 us (20%)
  other arithmetic  94.4 us (14%)
  matrix products  33.2 us (5%)
  between operations  14.5 us (2%)
    all_gather x1, waiting for transfers between devices, carried_in(): everything = jax.tree.map(lambda part: lax.all_gather(part, axis), x)  286 us
    unnamed x1, blocking collectives  123 us
    all_gather x1, waiting for transfers between devices, softmax_part(): value_piece = lax.all_gather(attn_value, 'ctx', axis=0, tiled=True)  109 us
    select_n x64, other arithmetic, hop(): return jax.tree.map(lambda a, b: jnp.where(reached, a, b), new, before)  75.1 us
    reduce_sum x1, other arithmetic, attend(): totals = jnp.sum(prob_rows, axis=2)  15.6 us
    dot_general x1, matrix products, attend(): jnp.einsum('gqp,pgd->gqd', prob_rows.astype(jnp.bfloat16), value_piece, p...  15.6 us
    dot_general x1, matrix products, attend(): jnp.einsum('gqd,pgd->gqp', group_query, key_piece, preferred_element_type...  15.5 us
  transfers between devices with their start and end apart: 3, of which 3 were waited for; matrix products, arithmetic and copies ran while one was open for 8% of the time, Pallas kernels for 0%

commit v1 on v0

--- a/solution.py
+++ b/solution.py
@@ -116,7 +116,9 @@
 
     initial = tuple((empty_state(query_set[0]) for query_set in query_sets))
     key_piece = lax.all_gather(attn_key, "ctx", axis=0, tiled=True)
-    value_piece = lax.all_gather(attn_value, "ctx", axis=0, tiled=True)
+    value_piece = jnp.concatenate(
+        lax.all_to_all(jnp.stack([attn_value] * lax.axis_size("ctx")), "ctx", 0, 0), axis=0
+    )
     results = []
     for query_set, state_now in zip(query_sets, initial):
         group_query, positions, set_rows = query_set

time: 693 us -> 576 us (0.83)
  waiting for transfers between devices: 406 us -> 187 us
  blocking collectives: 136 us -> 212 us
  starting transfers between devices: 0.11 us -> 19.4 us
    all_gather x1 -> x0, waiting for transfers between devices: 109 us -> none  [softmax_part(): value_piece = lax.all_gather(attn_value, 'ctx', axis=0, tiled=True)]
    all_gather x1, waiting for transfers between devices: 286 us -> 186 us  [carried_in(): everything = jax.tree.map(lambda part: lax.all_gather(part, axis), x)]
    unnamed x1, blocking collectives: 123 us -> 199 us
    all_to_all x0 -> x1, starting transfers between devices: none -> 19.3 us  [softmax_part(): lax.all_to_all(jnp.stack([attn_value] * lax.axis_size('ctx')), 'ctx', 0, 0)]
    all_gather x1, waiting for transfers between devices: 9.04 us -> 0.02 us  [softmax_part(): key_piece = lax.all_gather(attn_key, 'ctx', axis=0, tiled=True)]
  transfers between devices with their start and end apart: 3 -> 3, of which waited for: 3 -> 1; matrix products, arithmetic and copies ran while one was open for 8% -> 10% of each run, Pallas kernels for 0% -> 0%
where the time goes in v1:
time: 576 us; the launch traced here: 572 us
  blocking collectives  212 us (37%)
  waiting for transfers between devices  187 us (32%)
  other arithmetic  95.1 us (17%)
  matrix products  35.6 us (6%)
  starting transfers between devices  19.4 us (3%)
  between operations  14.8 us (3%)
  local copies, waits for them, and re-layouts  6.18 us (1%)
    unnamed x1, blocking collectives  199 us
    all_gather x1, waiting for transfers between devices, carried_in(): everything = jax.tree.map(lambda part: lax.all_gather(part, axis), x)  186 us
    select_n x64, other arithmetic, hop(): return jax.tree.map(lambda a, b: jnp.where(reached, a, b), new, before)  75.2 us
    all_to_all x1, starting transfers between devices, softmax_part(): lax.all_to_all(jnp.stack([attn_value] * lax.axis_size('ctx')), 'ctx', 0, 0)  19.3 us
    dot_general x1, matrix products, attend(): jnp.einsum('gqp,pgd->gqd', prob_rows.astype(jnp.bfloat16), value_piece, p...  16.9 us
    dot_general x1, matrix products, attend(): jnp.einsum('gqd,pgd->gqp', group_query, key_piece, preferred_element_type...  15.6 us
    reduce_sum x1, other arithmetic, attend(): totals = jnp.sum(prob_rows, axis=2)  15.6 us
    psum x1, blocking collectives, lightning(): total_squares = lax.psum(row_squares, 'head')  12.9 us
  transfers between devices with their start and end apart: 3, of which 1 were waited for; matrix products, arithmetic and copies ran while one was open for 10% of the time, Pallas kernels for 0%

profile of v1, /device:TPU:1, one launch (start us, length us, event | category | flops | bytes accessed | tf_op | source)
XLA Modules:
  0.0 572.4 jit_solution(5302320041468233618)
XLA Ops:
  9.3 1.9 multiply_convert_fusion.1
  12.3 2.6 stack.2
  14.9 19.3 %all-to-all-start = ((bf16[64,128,1,128]{3,1,2,0:T(8,128)(2,1)}), bf16[64,128,1,128]{3,1,2,0:T(8,128)(2,1)S(1)}, u32[]{:S(2)}, u32[]{:S(2)}) async-start(bf16[64,128,1,128]{3,1,2,0:T(8,128)(2,1)} %stack.2), calls=%async_computation | async-start | bytes 4194304 | tf_op jit(solution)/shard_map/all_to_all | solution.py:120
  34.2 1.3 dynamic-slice
  36.4 199.3 %all-reduce = f32[512]{0:T(512)S(1)} all-reduce(f32[512]{0:T(512)S(1)} %dynamic-update-slice), channel_id=2, replica_groups=mesh['ctx'=64,'head'=8] {'ctx'}, use_global_device_ids=true, to_apply=%add | all-reduce | flops 512 | bytes 4096
  237.1 15.6 %select_reduce_fusion = (f32[1024]{0:T(1024)S(1)}, f32[1024,8192]{1,0:T(8,128)}) fusion(s32[1024]{0:T(1024)S(1)} %ge.35, bf16[8192,1,128]{2,0,1:T(8,128)(2,1)} %all-gather.5.cloned.1.call-done, bf16[128,8,128]{2,1,0:T(8,128)(2,1)S(1)} %copy-done), kind=kOutput, calls=%fused_computation.4 | convolution fusion | flops 2181037056 | bytes 35921920 | tf_op jit(solution)/shard_map/gqd,pgd->gqp/dot_general | solution.py:83
  252.7 15.6 %fusion.1 = f32[1024]{0:T(1024)S(1)} fusion(f32[1024,8192]{1,0:T(8,128)} %get-tuple-element.140, f32[1024]{0:T(1024)S(1)} %broadcast_maximum_fusion, s32[1024]{0:T(1024)S(1)} %ge.35), kind=kLoop, calls=%fused_computation.6 | loop fusion | flops 41942016 | bytes 33566720 | tf_op jit(solution)/shard_map/reduce_sum | solution.py:91
  268.4 16.9 %fusion.16 = bf16[128,8,128]{2,1,0:T(8,128)(2,1)} fusion(bf16[8192,128]{1,0:T(8,128)(2,1)S(1)} %bitcast.40, f32[1024,8192]{1,0:T(8,128)} %get-tuple-element.140, f32[1024]{0:T(1024)S(1)} %broadcast_maximum_fusion, s32[1024]{0:T(1024)S(1)} %ge.35, f32[1024]{0:T(1024)S(1)} %fusion.1), kind=kOutput, calls=%fused_computation.19 | convolution fusion | flops 2189688832 | bytes 35926016 | tf_op jit(solution)/shard_map/gqp,pgd->gqd/dot_general | solution.py:92
  285.2 186.4 %all-gather.7.cloned.1.call-done = f32[512,128,128]{2,1,0:T(8,128)} async-done(((f32[8,128,128]{2,1,0:T(8,128)}), f32[512,128,128]{2,1,0:T(8,128)}) %all-gather.7.cloned.1.call-update) | async-done | bytes 33554448 | tf_op jit(solution)/shard_map/all_gather | solution.py:12
  471.6 77.9 %while.14 = (s32[]{:T(128)}, f32[8,128,128]{2,1,0:T(8,128)S(1)}, s32[]{:T(128)}, f32[64,8]{1,0:T(8,128)S(1)}, f32[64,8,128,128]{3,2,1,0:T(8,128)}, /*index=5*/s32[]{:T(128)}, s32[]{:T(128)}) while((s32[]{:T(128)}, f32[8,128,128]{2,1,0:T(8,128)S(1)}, s32[]{:T(128)}, f32[64,8]{1,0:T(8,128)S(1)}, f32[64,8,128,128]{3,2,1,0:T(8,128)}, ...), condition=%wide.region_2.3_spmd.clone, body=%wide.region_1.2_spmd.clone.sunk | while | flops 524292 | bytes 1573073 | solution.py:22
  472.8 1.2 fusion.59
  474.0 1.2 fusion.59
  475.3 1.2 fusion.59
  476.5 1.2 fusion.59
  477.7 1.2 fusion.59
  478.9 1.2 fusion.59
  480.1 1.2 fusion.59
  481.3 1.2 fusion.59
  482.6 1.2 fusion.59
  483.8 1.2 fusion.59
  485.0 1.2 fusion.59
  486.2 1.2 fusion.59
  487.4 1.2 fusion.59
  488.7 1.2 fusion.59
  489.9 1.2 fusion.59
  491.1 1.2 fusion.59
  492.3 1.2 fusion.59
  493.5 1.2 fusion.59
  494.7 1.2 fusion.59
  496.0 1.2 fusion.59
  497.2 1.2 fusion.59
  498.4 1.2 fusion.59
  499.6 1.2 fusion.59
  500.8 1.2 fusion.59
  502.0 1.2 fusion.59
  503.3 1.2 fusion.59
  504.5 1.2 fusion.59
  505.7 1.2 fusion.59
  506.9 1.2 fusion.59
  508.1 1.2 fusion.59
  509.4 1.2 fusion.59
  510.6 1.2 fusion.59
  511.8 1.2 fusion.59
  513.0 1.2 fusion.59
  514.2 1.2 fusion.59
  515.4 1.2 fusion.59
  516.7 1.2 fusion.59
  517.9 1.2 fusion.59
  519.1 1.2 fusion.59
  520.3 1.2 fusion.59
  521.5 1.2 fusion.59
  522.8 1.2 fusion.59
  525.2 1.2 fusion.59
  528.8 1.2 fusion.59
  530.1 1.2 fusion.59
  533.7 1.2 fusion.59
  534.9 1.2 fusion.59
  538.6 1.2 fusion.59
  539.8 1.2 fusion.59
  543.5 1.2 fusion.59
  544.7 1.2 fusion.59
  548.3 1.2 fusion.59
  550.1 1.5 multiply_reduce_fusion
  551.6 12.9 %psum.7 = f32[128]{0:T(128)S(1)} all-reduce(f32[128]{0:T(128)S(1)} %get-tuple-element.137), channel_id=1, replica_groups=mesh['ctx'=64,'head'=8] {'head'}, use_global_device_ids=true, to_apply=%region_4.5 | all-reduce | flops 128 | bytes 1024 | tf_op jit(solution)/shard_map/psum | solution.py:62
  (107 shorter events, 21.2 us)
Async XLA Ops:
  7.2 230.0 %copy-start = (bf16[128,8,128]{2,1,0:T(8,128)(2,1)S(1)}, bf16[128,8,128]{2,1,0:T(8,128)(2,1)}, u32[]{:S(2)}) copy-start(bf16[128,8,128]{2,1,0:T(8,128)(2,1)} %param.15) | copy-start | bytes 786436
  7.2 229.9 %all-gather.5.cloned.1.call-start = ((), (), s32[]{:S(2)}) async-start(), calls=%async_computation.1 | async-start | bytes 2129920 | tf_op jit(solution)/shard_map/all_gather | solution.py:118
  7.9 463.7 %all-gather.7.cloned.1.call-start = ((), (), s32[]{:S(2)}) async-start(), calls=%async_computation.2 | async-start | bytes 34078720 | tf_op jit(solution)/shard_map/all_gather | solution.py:12
  14.9 253.4 %all-to-all-start = ((bf16[64,128,1,128]{3,1,2,0:T(8,128)(2,1)}), bf16[64,128,1,128]{3,1,2,0:T(8,128)(2,1)S(1)}, u32[]{:S(2)}, u32[]{:S(2)}) async-start(bf16[64,128,1,128]{3,1,2,0:T(8,128)(2,1)} %stack.2), calls=%async_computation | async-start | bytes 4194304 | tf_op jit(solution)/shard_map/all_to_all | solution.py:120
  268.3 297.3 %copy-start.1 = (bf16[128,8,128]{2,1,0:T(8,128)(2,1)S(1)}, bf16[128,8,128]{2,1,0:T(8,128)(2,1)}, u32[]{:S(2)}) copy-start(bf16[128,8,128]{2,1,0:T(8,128)(2,1)} %param.15) | copy-start | bytes 786436
  268.3 296.1 %copy-start.2 = (f32[8,128]{1,0:T(8,128)S(1)}, f32[8,128]{1,0:T(8,128)}, u32[]{:S(2)}) copy-start(f32[8,128]{1,0:T(8,128)} %param.14) | copy-start | bytes 12292
Sparse Core Ops, SparseCore 0:
  11.0 159.0 all-gather.4
  173.0 298.5 all-gather.6
